TPU v7x, 256 devices: a whole 4x4x8 slice. The times are simulated.
256 devices in a mesh: pts: 128 (over y, x, z_lo, core), grp: 2 (over z_hi).
Axes of the slice: x: 4, y: 4, z: 8 (z_hi: 2, z_lo: 4; z = z_hi * 4 + z_lo), core: 2. Of those that a mesh axis runs over, the one named last changes fastest.
Arguments:
- grid_states: float32 [59, 2097152], P(None, ('pts', 'grp')), may hold values from 0 to 1
- coarse_active: int32 [16384, 8], P(('pts', 'grp')), may hold values from 0 to 127, all different within a row
- fine_active: int32 [16384, 8], P(('pts', 'grp')), may hold values from 0 to 31, all different within a row
- shock: int32 [2097152], P(('pts', 'grp')), may hold values from 0 to 3
- coarse_surplus: bfloat16 [4, 60, 16384], P(None, 'grp', 'pts'), may hold values from -0.796875 to 0.796875
- fine_surplus: bfloat16 [4, 60, 524288], P(None, 'grp', 'pts'), may hold values from -0.796875 to 0.796875
- coarse_dim: int32 [128], P('pts'), may hold values from 0 to 58
- coarse_level: int32 [128], P('pts'), may hold values from 0 to 2
- fine_dim: int32 [4096], P('pts'), may hold values from 0 to 58
- fine_level: int32 [4096], P('pts'), may hold values from 0 to 2
- tfp: float32 [4], replicated, may hold values from 0.5 to 2
- trans_weight: float32 [4, 4], replicated, may hold values from 0.2 to 5
Outputs:
- savings: bfloat16 [4, 60, 2097152], P(None, None, ('pts', 'grp'))
- prices: float32 [2, 2097152], P(None, ('pts', 'grp'))
Inputs may be any that keep to these rules, and one draw needn't show every extreme that they name: `coarse_active`: each row names 8 different coarse blocks, and every coarse block is named by some row. `fine_active`: each row names 8 different fine blocks of its region.
All inputs are finite; a program needn't handle non-finite values.
Results may differ from a plain program's by a relative error of at most 0.0034.
Values may be sent and summed in bfloat16 or wider, within the bound.
A program may use at most 128 MiB of HBM per device.

v0:
```python
import math
import jax
import jax.numpy as jnp
from jax import lax
from jax.sharding import PartitionSpec as P

S = 4
GEN = 60
BS = 128


def evaluate(states, active, table, dims_all, levels_all):
    nstate, npoints = states.shape
    tiles, nactive = active.shape
    tile = npoints // tiles
    block_size = table.shape[2]
    turns = math.gcd(tiles, 8)
    group = tiles // turns
    grouped = states.reshape(nstate, turns, group, tile).transpose(1, 2, 0, 3)
    active_grouped = active.reshape(turns, group, nactive)
    offsets = jnp.arange(block_size, dtype=jnp.float32)

    def one_tile(states_tile, block_ids):
        scales = (block_size - 1) * jnp.exp2(-levels_all[block_ids].astype(jnp.float32))
        scaled = scales[:, None] * states_tile[dims_all[block_ids]]
        phi = jnp.maximum(0.0, 1.0 - jnp.abs(scaled[:, None, :] - offsets[None, :, None])).astype(
            jnp.bfloat16
        )
        coef = table[block_ids]
        return jnp.einsum("kgj,kjt->gt", coef, phi, preferred_element_type=jnp.float32)

    def one_turn(pair):
        return jax.vmap(one_tile)(pair[0], pair[1])

    values = lax.map(one_turn, (grouped, active_grouped))
    return values.transpose(2, 0, 1, 3).reshape(table.shape[1], npoints)


def to_table(gathered):
    shocks, gens, basis = gathered.shape
    nblocks = basis // BS
    return gathered.reshape(shocks * gens, nblocks, BS).transpose(1, 0, 2)


def joined(coarse_all, fine_local, coarse_ids, fine_ids):
    table = jnp.concatenate([to_table(coarse_all), to_table(fine_local)], axis=0)
    ncoarse = coarse_all.shape[2] // BS
    ids = jnp.concatenate([coarse_ids, fine_ids + ncoarse], axis=1)
    return (table, ids)


def expected_prices(savings, shock, tfp, trans_weight):
    capital = jnp.mean(savings.astype(jnp.float32), axis=1)
    interest = 0.33 * tfp[:, None] * capital ** (0.33 - 1.0) + 1.0 - 0.1
    earnings = (1.0 - 0.33) * tfp[:, None] * capital**0.33
    transition = trans_weight / jnp.sum(trans_weight, axis=1, keepdims=True)
    onehot = (shock[None, :] == jnp.arange(S, dtype=jnp.int32)[:, None]).astype(jnp.float32)
    weights = jnp.dot(transition.T, onehot, precision=lax.Precision.HIGHEST)
    return jnp.stack([jnp.sum(weights * interest, axis=0), jnp.sum(weights * earnings, axis=0)])


def body(
    grid_states,
    coarse_active,
    fine_active,
    shock,
    coarse_surplus,
    fine_surplus,
    coarse_dim,
    coarse_level,
    fine_dim,
    fine_level,
    tfp,
    trans_weight,
):
    npoints = grid_states.shape[1]
    coarse_gens, fine_gens = (
        lax.all_gather(coarse_surplus, "grp", axis=1, tiled=True),
        lax.all_gather(fine_surplus, "grp", axis=1, tiled=True),
    )
    coarse_all, dims_coarse, levels_coarse = (
        lax.all_gather(coarse_gens, "pts", axis=2, tiled=True),
        lax.all_gather(coarse_dim, "pts", axis=0, tiled=True),
        lax.all_gather(coarse_level, "pts", axis=0, tiled=True),
    )
    table, block_ids = joined(coarse_all, fine_gens, coarse_active, fine_active)
    dims_all = jnp.concatenate([dims_coarse, fine_dim])
    levels_all = jnp.concatenate([levels_coarse, fine_level])
    log_savings = evaluate(grid_states, block_ids, table, dims_all, levels_all)
    savings = jnp.exp(log_savings).astype(jnp.bfloat16).reshape(S, GEN, npoints)
    prices = expected_prices(savings, shock, tfp, trans_weight)
    return (savings, prices)


def solution(mesh):
    in_specs = (
        P(None, ("pts", "grp")),
        P(("pts", "grp"), None),
        P(("pts", "grp"), None),
        P(("pts", "grp")),
        P(None, "grp", "pts"),
        P(None, "grp", "pts"),
        P("pts"),
        P("pts"),
        P("pts"),
        P("pts"),
        P(),
        P(),
    )
    out_specs = (P(None, None, ("pts", "grp")), P(None, ("pts", "grp")))
    return jax.shard_map(body, mesh=mesh, in_specs=in_specs, out_specs=out_specs, check_vma=False)
```

profile of v0, /device:TPU:1, one launch (start us, length us, event | category | flops | bytes accessed | tf_op | source)
XLA Modules:
  0.0 540.3 jit_solution(2822092789721412001)
XLA Ops:
  7.9 11.4 %all_gather.15 = bf16[4,60,128]{2,0,1:T(4,128)(2,1)} all-gather(bf16[4,30,128]{2,0,1:T(4,128)(2,1)} %param.18), channel_id=1, replica_groups=mesh['pts'=128,'grp'=2] {'grp'}, dimensions={1}, use_global_device_ids=true | all-gather | bytes 92160 | tf_op jit(solution)/shard_map/all_gather | solution.py:78
  27.8 21.5 %all-reduce.2 = (s32[128]{0:T(128)S(1)}, s32[128]{0:T(128)S(1)}) all-reduce(s32[128]{0:T(128)S(1)} %dynamic-update-slice, s32[128]{0:T(128)S(1)} %dynamic-update-slice.1), channel_id=1, replica_groups=mesh['pts'=128,'grp'=2] {'pts'}, use_global_device_ids=true, to_apply=%add | all-reduce | flops 256 | bytes 2048
  52.1 23.6 %all-gather.5.cloned.1.call-done = bf16[4,60,4096]{2,0,1:T(4,128)(2,1)} async-done(((bf16[4,30,4096]{2,0,1:T(4,128)(2,1)}), bf16[4,60,4096]{2,0,1:T(4,128)(2,1)}) %all-gather.5.cloned.1.call-update) | async-done | bytes 1966096 | tf_op jit(solution)/shard_map/all_gather | solution.py:79
  80.4 214.3 %all-gather.3.cloned.1.call-done = bf16[4,60,16384]{2,0,1:T(4,128)(2,1)} async-done(((bf16[4,60,128]{2,0,1:T(4,128)(2,1)}), bf16[4,60,16384]{2,0,1:T(4,128)(2,1)}) %all-gather.3.cloned.1.call-update) | async-done | bytes 7864336 | tf_op jit(solution)/shard_map/all_gather | solution.py:82
  294.6 10.9 %copy.23 = bf16[4,60,16384]{2,1,0:T(8,128)(2,1)} copy(bf16[4,60,16384]{2,0,1:T(4,128)(2,1)} %all-gather.3.cloned.1.call-done) | data formatting | bytes 15728640 | tf_op jit(solution)/shard_map/all_gather | solution.py:82
  305.5 9.1 %reshape.80 = bf16[240,128,128]{2,1,0:T(8,128)(2,1)} reshape(bf16[4,60,16384]{2,1,0:T(8,128)(2,1)} %copy.23) | data formatting | bytes 15728640 | tf_op jit(solution)/shard_map/reshape | solution.py:42
  314.6 8.5 %pad_maximum_fusion = bf16[160,240,128]{2,0,1:T(8,128)(2,1)} fusion(bf16[32,240,128]{2,0,1:T(8,128)(2,1)S(1)} %bitcast.50, bf16[128,240,128]{2,0,1:T(8,128)(2,1)} %bitcast.49), kind=kLoop, calls=%fused_computation.27 | loop fusion | flops 19660800 | bytes 19660800 | tf_op jit(solution)/shard_map/concatenate | solution.py:46
  323.1 11.3 %copy.25 = bf16[160,240,128]{2,1,0:T(8,128)(2,1)} copy(bf16[160,240,128]{2,0,1:T(8,128)(2,1)} %pad_maximum_fusion) | data formatting | bytes 19660800
  334.5 174.7 %while.11 = (s32[]{:T(128)}, f32[8,8,240,128]{3,2,1,0:T(8,128)}, s32[8,8,16]{2,1,0:T(8,128)S(1)}, bf16[160,240,128]{2,1,0:T(8,128)(2,1)}, s32[160]{0:T(256)S(1)}...) while((s32[]{:T(128)}, f32[8,8,240,128]{3,2,1,0:T(8,128)}, ...), condition=%wide.region_1.2_spmd.clone, body=%wide.region_0.1_spmd.clone.sunk | while | flops 1017138048 | bytes 25404508 | solution.py:35
  339.4 10.4 %gather_fusion = bf16[128,240,128]{2,1,0:T(8,128)(2,1)} fusion(bf16[160,240,128]{2,1,0:T(8,128)(2,1)} %get-tuple-element.163, s32[1024]{0:T(1024)S(1)} %pad_clamp_fusion.2), kind=kCustom, calls=%fused_computation.clone.clone.1 | custom fusion | bytes 15729152 | tf_op jit(solution)/shard_map/while/body/eval_jaxpr/vmap()/gather | solution.py:29
  361.2 10.4 %gather_fusion = bf16[128,240,128]{2,1,0:T(8,128)(2,1)} fusion(bf16[160,240,128]{2,1,0:T(8,128)(2,1)} %get-tuple-element.163, s32[1024]{0:T(1024)S(1)} %pad_clamp_fusion.2), kind=kCustom, calls=%fused_computation.clone.clone.1 | custom fusion | bytes 15729152 | tf_op jit(solution)/shard_map/while/body/eval_jaxpr/vmap()/gather | solution.py:29
  371.6 6.5 %fusion.35 = f32[8,8,240,128]{3,2,1,0:T(8,128)} fusion(f32[8,8,240,128]{3,2,1,0:T(8,128)} %get-tuple-element.153, s32[]{:T(128)} %get-tuple-element.152, bf16[8,16,240,128]{3,2,1,0:T(8,128)(2,1)} %bitcast.48, f32[8,16,128]{2,1,0:T(8,128)S(1)} %broadcast_multiply_fusion.4), kind=kOutput, calls=%fused_computation.15.clone.1 | convolution fusion | flops 1017118720 | bytes 8913408 | tf_op jit(solution)/shard_map/while/body/eval_jaxpr/vmap(kgj,kjt->gt)/dot_general | solution.py:30
  383.1 10.4 %gather_fusion = bf16[128,240,128]{2,1,0:T(8,128)(2,1)} fusion(bf16[160,240,128]{2,1,0:T(8,128)(2,1)} %get-tuple-element.163, s32[1024]{0:T(1024)S(1)} %pad_clamp_fusion.2), kind=kCustom, calls=%fused_computation.clone.clone.1 | custom fusion | bytes 15729152 | tf_op jit(solution)/shard_map/while/body/eval_jaxpr/vmap()/gather | solution.py:29
  393.5 6.5 %fusion.35 = f32[8,8,240,128]{3,2,1,0:T(8,128)} fusion(f32[8,8,240,128]{3,2,1,0:T(8,128)} %get-tuple-element.153, s32[]{:T(128)} %get-tuple-element.152, bf16[8,16,240,128]{3,2,1,0:T(8,128)(2,1)} %bitcast.48, f32[8,16,128]{2,1,0:T(8,128)S(1)} %broadcast_multiply_fusion.4), kind=kOutput, calls=%fused_computation.15.clone.1 | convolution fusion | flops 1017118720 | bytes 8913408 | tf_op jit(solution)/shard_map/while/body/eval_jaxpr/vmap(kgj,kjt->gt)/dot_general | solution.py:30
  404.9 10.4 %gather_fusion = bf16[128,240,128]{2,1,0:T(8,128)(2,1)} fusion(bf16[160,240,128]{2,1,0:T(8,128)(2,1)} %get-tuple-element.163, s32[1024]{0:T(1024)S(1)} %pad_clamp_fusion.2), kind=kCustom, calls=%fused_computation.clone.clone.1 | custom fusion | bytes 15729152 | tf_op jit(solution)/shard_map/while/body/eval_jaxpr/vmap()/gather | solution.py:29
  415.3 6.5 %fusion.35 = f32[8,8,240,128]{3,2,1,0:T(8,128)} fusion(f32[8,8,240,128]{3,2,1,0:T(8,128)} %get-tuple-element.153, s32[]{:T(128)} %get-tuple-element.152, bf16[8,16,240,128]{3,2,1,0:T(8,128)(2,1)} %bitcast.48, f32[8,16,128]{2,1,0:T(8,128)S(1)} %broadcast_multiply_fusion.4), kind=kOutput, calls=%fused_computation.15.clone.1 | convolution fusion | flops 1017118720 | bytes 8913408 | tf_op jit(solution)/shard_map/while/body/eval_jaxpr/vmap(kgj,kjt->gt)/dot_general | solution.py:30
  426.7 10.4 %gather_fusion = bf16[128,240,128]{2,1,0:T(8,128)(2,1)} fusion(bf16[160,240,128]{2,1,0:T(8,128)(2,1)} %get-tuple-element.163, s32[1024]{0:T(1024)S(1)} %pad_clamp_fusion.2), kind=kCustom, calls=%fused_computation.clone.clone.1 | custom fusion | bytes 15729152 | tf_op jit(solution)/shard_map/while/body/eval_jaxpr/vmap()/gather | solution.py:29
  437.2 6.5 %fusion.35 = f32[8,8,240,128]{3,2,1,0:T(8,128)} fusion(f32[8,8,240,128]{3,2,1,0:T(8,128)} %get-tuple-element.153, s32[]{:T(128)} %get-tuple-element.152, bf16[8,16,240,128]{3,2,1,0:T(8,128)(2,1)} %bitcast.48, f32[8,16,128]{2,1,0:T(8,128)S(1)} %broadcast_multiply_fusion.4), kind=kOutput, calls=%fused_computation.15.clone.1 | convolution fusion | flops 1017118720 | bytes 8913408 | tf_op jit(solution)/shard_map/while/body/eval_jaxpr/vmap(kgj,kjt->gt)/dot_general | solution.py:30
  448.6 10.4 %gather_fusion = bf16[128,240,128]{2,1,0:T(8,128)(2,1)} fusion(bf16[160,240,128]{2,1,0:T(8,128)(2,1)} %get-tuple-element.163, s32[1024]{0:T(1024)S(1)} %pad_clamp_fusion.2), kind=kCustom, calls=%fused_computation.clone.clone.1 | custom fusion | bytes 15729152 | tf_op jit(solution)/shard_map/while/body/eval_jaxpr/vmap()/gather | solution.py:29
  459.0 6.5 %fusion.35 = f32[8,8,240,128]{3,2,1,0:T(8,128)} fusion(f32[8,8,240,128]{3,2,1,0:T(8,128)} %get-tuple-element.153, s32[]{:T(128)} %get-tuple-element.152, bf16[8,16,240,128]{3,2,1,0:T(8,128)(2,1)} %bitcast.48, f32[8,16,128]{2,1,0:T(8,128)S(1)} %broadcast_multiply_fusion.4), kind=kOutput, calls=%fused_computation.15.clone.1 | convolution fusion | flops 1017118720 | bytes 8913408 | tf_op jit(solution)/shard_map/while/body/eval_jaxpr/vmap(kgj,kjt->gt)/dot_general | solution.py:30
  470.4 10.4 %gather_fusion = bf16[128,240,128]{2,1,0:T(8,128)(2,1)} fusion(bf16[160,240,128]{2,1,0:T(8,128)(2,1)} %get-tuple-element.163, s32[1024]{0:T(1024)S(1)} %pad_clamp_fusion.2), kind=kCustom, calls=%fused_computation.clone.clone.1 | custom fusion | bytes 15729152 | tf_op jit(solution)/shard_map/while/body/eval_jaxpr/vmap()/gather | solution.py:29
  480.9 6.5 %fusion.35 = f32[8,8,240,128]{3,2,1,0:T(8,128)} fusion(f32[8,8,240,128]{3,2,1,0:T(8,128)} %get-tuple-element.153, s32[]{:T(128)} %get-tuple-element.152, bf16[8,16,240,128]{3,2,1,0:T(8,128)(2,1)} %bitcast.48, f32[8,16,128]{2,1,0:T(8,128)S(1)} %broadcast_multiply_fusion.4), kind=kOutput, calls=%fused_computation.15.clone.1 | convolution fusion | flops 1017118720 | bytes 8913408 | tf_op jit(solution)/shard_map/while/body/eval_jaxpr/vmap(kgj,kjt->gt)/dot_general | solution.py:30
  492.3 10.4 %gather_fusion = bf16[128,240,128]{2,1,0:T(8,128)(2,1)} fusion(bf16[160,240,128]{2,1,0:T(8,128)(2,1)} %get-tuple-element.163, s32[1024]{0:T(1024)S(1)} %pad_clamp_fusion.2), kind=kCustom, calls=%fused_computation.clone.clone.1 | custom fusion | bytes 15729152 | tf_op jit(solution)/shard_map/while/body/eval_jaxpr/vmap()/gather | solution.py:29
  524.9 7.1 %copy.28 = bf16[4,60,8192]{2,0,1:T(4,128)(2,1)} copy(bf16[4,60,8192]{2,1,0:T(8,128)(2,1)} %convert_element_type.26) | data formatting | bytes 7864320
  (138 shorter events, 84.4 us)
Async XLA Ops:
  7.2 68.6 %all-gather.5.cloned.1.call-start = ((), (), s32[]{:S(2)}) async-start(), calls=%async_computation.1 | async-start | bytes 2949120 | tf_op jit(solution)/shard_map/all_gather | solution.py:79
  7.9 286.7 %all-gather.3.cloned.1.call-start = ((), (), s32[]{:S(2)}) async-start(), calls=%async_computation | async-start | bytes 7925760 | tf_op jit(solution)/shard_map/all_gather | solution.py:82
  305.5 9.1 %copy-start = (bf16[240,32,128]{2,1,0:T(8,128)(2,1)S(1)}, bf16[240,32,128]{2,1,0:T(8,128)(2,1)}, u32[]{:S(2)}) copy-start(bf16[240,32,128]{2,1,0:T(8,128)(2,1)} %reshape.81) | copy-start | bytes 5898244
  521.9 10.2 %copy-start.1 = (f32[4,4]{1,0:T(4,128)S(1)}, f32[4,4]{1,0:T(4,128)}, u32[]{:S(2)}) copy-start(f32[4,4]{1,0:T(4,128)} %param.25) | copy-start | bytes 196
  521.9 10.2 %copy-start.2 = (s32[8192]{0:T(1024)S(1)}, s32[8192]{0:T(1024)}, u32[]{:S(2)}) copy-start(s32[8192]{0:T(1024)} %param.17) | copy-start | bytes 98308
Sparse Core Ops, SparseCore 0:
  9.8 65.9 all-gather.4
  77.5 217.0 all-gather.2
where the time goes:
time: 542 us; the launch traced here: 540 us
  waiting for transfers between devices  239 us (44%)
  local copies, waits for them, and re-layouts  180 us (33%)
  matrix products  52.4 us (10%)
  blocking collectives  33 us (6%)
  other arithmetic  20.9 us (4%)
  between operations  15.4 us (3%)
    all_gather x1, waiting for transfers between devices, body(): lax.all_gather(coarse_gens, 'pts', axis=2, tiled=True)  214 us
    gather x8, local copies, waits for them, and re-layouts, one_tile(): coef = table[block_ids]  83.5 us
    dot_general x8, matrix products, one_tile(): jnp.einsum('kgj,kjt->gt', coef, phi, preferred_element_type=jnp.float32)  51.7 us
    all_gather x1, waiting for transfers between devices, body(): lax.all_gather(fine_surplus, 'grp', axis=1, tiled=True)  23.6 us
    unnamed x14, local copies, waits for them, and re-layouts  23.3 us
    unnamed x1, blocking collectives  21.5 us
    gather x32, local copies, waits for them, and re-layouts, one_tile(): scaled = scales[:, None] * states_tile[dims_all[block_ids]]  19.1 us
    all_gather x1, blocking collectives, body(): lax.all_gather(coarse_surplus, 'grp', axis=1, tiled=True)  11.4 us
  transfers between devices with their start and end apart: 2, of which 2 were waited for; matrix products, arithmetic and copies ran while one was open for 3% of the time, Pallas kernels for 0%

commit v1 on v0

--- a/solution.py
+++ b/solution.py
@@ -78,8 +78,18 @@
         lax.all_gather(coarse_surplus, "grp", axis=1, tiled=True),
         lax.all_gather(fine_surplus, "grp", axis=1, tiled=True),
     )
+
+    def get_row(obj):
+        ledger = []
+        for _ in range(lax.axis_size("pts")):
+            ledger.append(obj)
+        return jnp.concatenate(
+            lax.all_to_all(jnp.stack(ledger, axis=0), axis_name="pts", split_axis=0, concat_axis=0),
+            axis=2,
+        )
+
     coarse_all, dims_coarse, levels_coarse = (
-        lax.all_gather(coarse_gens, "pts", axis=2, tiled=True),
+        get_row(coarse_gens),
         lax.all_gather(coarse_dim, "pts", axis=0, tiled=True),
         lax.all_gather(coarse_level, "pts", axis=0, tiled=True),
     )

time: 542 us -> 503 us (0.928)
  waiting for transfers between devices: 239 us -> 0.68 us
  blocking collectives: 33 us -> 228 us
  starting transfers between devices: 0.08 us -> 13.2 us
  local copies, waits for them, and re-layouts: 180 us -> 172 us
    all_gather x1 -> x0, waiting for transfers between devices: 214 us -> none  [body(): lax.all_gather(coarse_gens, 'pts', axis=2, tiled=True)]
    unnamed x1, blocking collectives: 21.5 us -> 219 us
    all_gather x1, waiting for transfers between devices: 23.6 us -> 0.01 us  [body(): lax.all_gather(fine_surplus, 'grp', axis=1, tiled=True)]
    all_to_all x0 -> x1, starting transfers between devices: none -> 13.1 us  [get_row(): lax.all_to_all(jnp.stack(ledger, axis=0), axis_name='pts', split_axis=0,...]
    all_gather x1 -> x0, local copies, waits for them, and re-layouts: 10.9 us -> none  [body(): lax.all_gather(coarse_gens, 'pts', axis=2, tiled=True)]
    reshape x2 -> x1, local copies, waits for them, and re-layouts: 11.1 us -> 1.99 us  [to_table(): return gathered.reshape(shocks * gens, nblocks, BS).transpose(1, 0, 2)]
    all_to_all x0 -> x1, local copies, waits for them, and re-layouts: none -> 8.57 us  [get_row(): lax.all_to_all(jnp.stack(ledger, axis=0), axis_name='pts', split_axis=0,...]
    unnamed x14 -> x26, local copies, waits for them, and re-layouts: 23.3 us -> 22.6 us
  transfers between devices with their start and end apart: 2 -> 2, of which waited for: 2 -> 0; matrix products, arithmetic and copies ran while one was open for 3% -> 2% of each run, Pallas kernels for 0% -> 0%
where the time goes in v1:
time: 503 us; the launch traced here: 500 us
  blocking collectives  228 us (45%)
  local copies, waits for them, and re-layouts  172 us (34%)
  matrix products  52.6 us (10%)
  other arithmetic  17.6 us (3%)
  between operations  15.5 us (3%)
  starting transfers between devices  13.2 us (3%)
    unnamed x1, blocking collectives  219 us
    gather x8, local copies, waits for them, and re-layouts, one_tile(): coef = table[block_ids]  83 us
    dot_general x8, matrix products, one_tile(): jnp.einsum('kgj,kjt->gt', coef, phi, preferred_element_type=jnp.float32)  51.9 us
    unnamed x26, local copies, waits for them, and re-layouts  22.6 us
    gather x32, local copies, waits for them, and re-layouts, one_tile(): scaled = scales[:, None] * states_tile[dims_all[block_ids]]  19.1 us
    all_to_all x1, starting transfers between devices, get_row(): lax.all_to_all(jnp.stack(ledger, axis=0), axis_name='pts', split_axis=0,...  13.1 us
    gather x8, local copies, waits for them, and re-layouts, one_tile(): levels_all[block_ids].astype(jnp.float32)  10.1 us
  transfers between devices with their start and end apart: 2, of which 0 were waited for; matrix products, arithmetic and copies ran while one was open for 2% of the time, Pallas kernels for 0%

profile of v1, /device:TPU:1, one launch (start us, length us, event | category | flops | bytes accessed | tf_op | source)
XLA Modules:
  0.0 500.4 jit_solution(787861838879649505)
XLA Ops:
  7.2 9.9 %all_gather.12 = bf16[4,60,128]{2,0,1:T(4,128)(2,1)S(1)} all-gather(bf16[4,30,128]{2,0,1:T(4,128)(2,1)} %param.18), channel_id=1, replica_groups=mesh['pts'=128,'grp'=2] {'grp'}, dimensions={1}, use_global_device_ids=true | all-gather | bytes 92160 | tf_op jit(solution)/shard_map/all_gather | solution.py:78
  22.3 13.1 %all-to-all-start = ((bf16[128,4,60,128]{3,1,2,0:T(4,128)(2,1)}), bf16[128,4,60,128]{3,1,2,0:T(4,128)(2,1)}, u32[]{:S(2)}, u32[]{:S(2)}) async-start(bf16[128,4,60,128]{3,1,2,0:T(4,128)(2,1)} %stack.8), calls=%async_computation | async-start | bytes 15728640 | tf_op jit(solution)/shard_map/all_to_all | solution.py:87
  41.8 218.5 %all-reduce.2 = (s32[128]{0:T(128)S(1)}, s32[128]{0:T(128)S(1)}) all-reduce(s32[128]{0:T(128)S(1)} %dynamic-update-slice, s32[128]{0:T(128)S(1)} %dynamic-update-slice.1), channel_id=1, replica_groups=mesh['pts'=128,'grp'=2] {'pts'}, use_global_device_ids=true, to_apply=%add | all-reduce | flops 256 | bytes 2048
  266.4 8.6 %copy.32 = bf16[128,4,60,128]{3,0,2,1:T(8,128)(2,1)} copy(bf16[128,4,60,128]{3,1,2,0:T(4,128)(2,1)} %all-to-all-done) | data formatting | bytes 15728640 | tf_op jit(solution)/shard_map/all_to_all | solution.py:87
  275.0 8.5 %pad_maximum_fusion = bf16[160,240,128]{2,0,1:T(8,128)(2,1)} fusion(bf16[32,240,128]{2,0,1:T(8,128)(2,1)S(1)} %bitcast.54, bf16[128,240,128]{2,0,1:T(8,128)(2,1)} %bitcast.53), kind=kLoop, calls=%fused_computation.27 | loop fusion | flops 19660800 | bytes 19660800 | tf_op jit(solution)/shard_map/concatenate | solution.py:46
  283.5 11.4 %copy.34 = bf16[160,240,128]{2,1,0:T(8,128)(2,1)} copy(bf16[160,240,128]{2,0,1:T(8,128)(2,1)} %pad_maximum_fusion) | data formatting | bytes 19660800
  294.9 174.4 %while.11 = (s32[]{:T(128)}, f32[8,8,240,128]{3,2,1,0:T(8,128)}, s32[8,8,16]{2,1,0:T(8,128)S(1)}, bf16[160,240,128]{2,1,0:T(8,128)(2,1)}, s32[160]{0:T(256)S(1)}...) while((s32[]{:T(128)}, f32[8,8,240,128]{3,2,1,0:T(8,128)}, ...), condition=%wide.region_1.2_spmd.clone, body=%wide.region_0.1_spmd.clone.sunk | while | flops 1017138048 | bytes 25404508 | solution.py:35
  299.8 10.4 %gather_fusion = bf16[128,240,128]{2,1,0:T(8,128)(2,1)} fusion(bf16[160,240,128]{2,1,0:T(8,128)(2,1)} %get-tuple-element.172, s32[1024]{0:T(1024)S(1)} %pad_clamp_fusion.2), kind=kCustom, calls=%fused_computation.clone.clone.1 | custom fusion | bytes 15729152 | tf_op jit(solution)/shard_map/while/body/eval_jaxpr/vmap()/gather | solution.py:29
  310.2 6.4 %fusion.35 = f32[8,8,240,128]{3,2,1,0:T(8,128)} fusion(f32[8,8,240,128]{3,2,1,0:T(8,128)} %get-tuple-element.162, s32[]{:T(128)} %get-tuple-element.161, bf16[8,16,240,128]{3,2,1,0:T(8,128)(2,1)} %bitcast.52, f32[8,16,128]{2,1,0:T(8,128)S(1)} %broadcast_multiply_fusion.4), kind=kOutput, calls=%fused_computation.15.clone.1 | convolution fusion | flops 1017118720 | bytes 8913408 | tf_op jit(solution)/shard_map/while/body/eval_jaxpr/vmap(kgj,kjt->gt)/dot_general | solution.py:30
  321.6 10.4 %gather_fusion = bf16[128,240,128]{2,1,0:T(8,128)(2,1)} fusion(bf16[160,240,128]{2,1,0:T(8,128)(2,1)} %get-tuple-element.172, s32[1024]{0:T(1024)S(1)} %pad_clamp_fusion.2), kind=kCustom, calls=%fused_computation.clone.clone.1 | custom fusion | bytes 15729152 | tf_op jit(solution)/shard_map/while/body/eval_jaxpr/vmap()/gather | solution.py:29
  331.9 6.5 %fusion.35 = f32[8,8,240,128]{3,2,1,0:T(8,128)} fusion(f32[8,8,240,128]{3,2,1,0:T(8,128)} %get-tuple-element.162, s32[]{:T(128)} %get-tuple-element.161, bf16[8,16,240,128]{3,2,1,0:T(8,128)(2,1)} %bitcast.52, f32[8,16,128]{2,1,0:T(8,128)S(1)} %broadcast_multiply_fusion.4), kind=kOutput, calls=%fused_computation.15.clone.1 | convolution fusion | flops 1017118720 | bytes 8913408 | tf_op jit(solution)/shard_map/while/body/eval_jaxpr/vmap(kgj,kjt->gt)/dot_general | solution.py:30
  343.3 10.4 %gather_fusion = bf16[128,240,128]{2,1,0:T(8,128)(2,1)} fusion(bf16[160,240,128]{2,1,0:T(8,128)(2,1)} %get-tuple-element.172, s32[1024]{0:T(1024)S(1)} %pad_clamp_fusion.2), kind=kCustom, calls=%fused_computation.clone.clone.1 | custom fusion | bytes 15729152 | tf_op jit(solution)/shard_map/while/body/eval_jaxpr/vmap()/gather | solution.py:29
  353.7 6.5 %fusion.35 = f32[8,8,240,128]{3,2,1,0:T(8,128)} fusion(f32[8,8,240,128]{3,2,1,0:T(8,128)} %get-tuple-element.162, s32[]{:T(128)} %get-tuple-element.161, bf16[8,16,240,128]{3,2,1,0:T(8,128)(2,1)} %bitcast.52, f32[8,16,128]{2,1,0:T(8,128)S(1)} %broadcast_multiply_fusion.4), kind=kOutput, calls=%fused_computation.15.clone.1 | convolution fusion | flops 1017118720 | bytes 8913408 | tf_op jit(solution)/shard_map/while/body/eval_jaxpr/vmap(kgj,kjt->gt)/dot_general | solution.py:30
  365.1 10.4 %gather_fusion = bf16[128,240,128]{2,1,0:T(8,128)(2,1)} fusion(bf16[160,240,128]{2,1,0:T(8,128)(2,1)} %get-tuple-element.172, s32[1024]{0:T(1024)S(1)} %pad_clamp_fusion.2), kind=kCustom, calls=%fused_computation.clone.clone.1 | custom fusion | bytes 15729152 | tf_op jit(solution)/shard_map/while/body/eval_jaxpr/vmap()/gather | solution.py:29
  375.5 6.5 %fusion.35 = f32[8,8,240,128]{3,2,1,0:T(8,128)} fusion(f32[8,8,240,128]{3,2,1,0:T(8,128)} %get-tuple-element.162, s32[]{:T(128)} %get-tuple-element.161, bf16[8,16,240,128]{3,2,1,0:T(8,128)(2,1)} %bitcast.52, f32[8,16,128]{2,1,0:T(8,128)S(1)} %broadcast_multiply_fusion.4), kind=kOutput, calls=%fused_computation.15.clone.1 | convolution fusion | flops 1017118720 | bytes 8913408 | tf_op jit(solution)/shard_map/while/body/eval_jaxpr/vmap(kgj,kjt->gt)/dot_general | solution.py:30
  386.9 10.4 %gather_fusion = bf16[128,240,128]{2,1,0:T(8,128)(2,1)} fusion(bf16[160,240,128]{2,1,0:T(8,128)(2,1)} %get-tuple-element.172, s32[1024]{0:T(1024)S(1)} %pad_clamp_fusion.2), kind=kCustom, calls=%fused_computation.clone.clone.1 | custom fusion | bytes 15729152 | tf_op jit(solution)/shard_map/while/body/eval_jaxpr/vmap()/gather | solution.py:29
  397.3 6.4 %fusion.35 = f32[8,8,240,128]{3,2,1,0:T(8,128)} fusion(f32[8,8,240,128]{3,2,1,0:T(8,128)} %get-tuple-element.162, s32[]{:T(128)} %get-tuple-element.161, bf16[8,16,240,128]{3,2,1,0:T(8,128)(2,1)} %bitcast.52, f32[8,16,128]{2,1,0:T(8,128)S(1)} %broadcast_multiply_fusion.4), kind=kOutput, calls=%fused_computation.15.clone.1 | convolution fusion | flops 1017118720 | bytes 8913408 | tf_op jit(solution)/shard_map/while/body/eval_jaxpr/vmap(kgj,kjt->gt)/dot_general | solution.py:30
  408.6 10.4 %gather_fusion = bf16[128,240,128]{2,1,0:T(8,128)(2,1)} fusion(bf16[160,240,128]{2,1,0:T(8,128)(2,1)} %get-tuple-element.172, s32[1024]{0:T(1024)S(1)} %pad_clamp_fusion.2), kind=kCustom, calls=%fused_computation.clone.clone.1 | custom fusion | bytes 15729152 | tf_op jit(solution)/shard_map/while/body/eval_jaxpr/vmap()/gather | solution.py:29
  419.0 6.6 %fusion.35 = f32[8,8,240,128]{3,2,1,0:T(8,128)} fusion(f32[8,8,240,128]{3,2,1,0:T(8,128)} %get-tuple-element.162, s32[]{:T(128)} %get-tuple-element.161, bf16[8,16,240,128]{3,2,1,0:T(8,128)(2,1)} %bitcast.52, f32[8,16,128]{2,1,0:T(8,128)S(1)} %broadcast_multiply_fusion.4), kind=kOutput, calls=%fused_computation.15.clone.1 | convolution fusion | flops 1017118720 | bytes 8913408 | tf_op jit(solution)/shard_map/while/body/eval_jaxpr/vmap(kgj,kjt->gt)/dot_general | solution.py:30
  430.5 10.4 %gather_fusion = bf16[128,240,128]{2,1,0:T(8,128)(2,1)} fusion(bf16[160,240,128]{2,1,0:T(8,128)(2,1)} %get-tuple-element.172, s32[1024]{0:T(1024)S(1)} %pad_clamp_fusion.2), kind=kCustom, calls=%fused_computation.clone.clone.1 | custom fusion | bytes 15729152 | tf_op jit(solution)/shard_map/while/body/eval_jaxpr/vmap()/gather | solution.py:29
  440.9 6.5 %fusion.35 = f32[8,8,240,128]{3,2,1,0:T(8,128)} fusion(f32[8,8,240,128]{3,2,1,0:T(8,128)} %get-tuple-element.162, s32[]{:T(128)} %get-tuple-element.161, bf16[8,16,240,128]{3,2,1,0:T(8,128)(2,1)} %bitcast.52, f32[8,16,128]{2,1,0:T(8,128)S(1)} %broadcast_multiply_fusion.4), kind=kOutput, calls=%fused_computation.15.clone.1 | convolution fusion | flops 1017118720 | bytes 8913408 | tf_op jit(solution)/shard_map/while/body/eval_jaxpr/vmap(kgj,kjt->gt)/dot_general | solution.py:30
  452.4 10.4 %gather_fusion = bf16[128,240,128]{2,1,0:T(8,128)(2,1)} fusion(bf16[160,240,128]{2,1,0:T(8,128)(2,1)} %get-tuple-element.172, s32[1024]{0:T(1024)S(1)} %pad_clamp_fusion.2), kind=kCustom, calls=%fused_computation.clone.clone.1 | custom fusion | bytes 15729152 | tf_op jit(solution)/shard_map/while/body/eval_jaxpr/vmap()/gather | solution.py:29
  462.8 6.5 %fusion.35 = f32[8,8,240,128]{3,2,1,0:T(8,128)} fusion(f32[8,8,240,128]{3,2,1,0:T(8,128)} %get-tuple-element.162, s32[]{:T(128)} %get-tuple-element.161, bf16[8,16,240,128]{3,2,1,0:T(8,128)(2,1)} %bitcast.52, f32[8,16,128]{2,1,0:T(8,128)S(1)} %broadcast_multiply_fusion.4), kind=kOutput, calls=%fused_computation.15.clone.1 | convolution fusion | flops 1017118720 | bytes 8913408 | tf_op jit(solution)/shard_map/while/body/eval_jaxpr/vmap(kgj,kjt->gt)/dot_general | solution.py:30
  485.0 7.1 %copy.37 = bf16[4,60,8192]{2,0,1:T(4,128)(2,1)} copy(bf16[4,60,8192]{2,1,0:T(8,128)(2,1)} %convert_element_type.26) | data formatting | bytes 7864320
  (149 shorter events, 72.6 us)
Async XLA Ops:
  22.3 17.2 %copy-start.1 = (s32[64,8]{0,1:T(8,128)S(1)}, s32[64,8]{0,1:T(8,128)}, u32[]{:S(2)}) copy-start(s32[64,8]{0,1:T(8,128)} %param.16) | copy-start | bytes 6148
  22.3 17.2 %copy-start.2 = (s32[64,8]{0,1:T(8,128)S(1)}, s32[64,8]{0,1:T(8,128)}, u32[]{:S(2)}) copy-start(s32[64,8]{0,1:T(8,128)} %param.15) | copy-start | bytes 6148
  22.3 17.3 %copy-start.8 = (u32[256]{0:T(256)S(1)}, u32[256]{0:T(256)}, u32[]{:S(2)}) copy-start(u32[256]{0:T(256)} %constant.67) | copy-start | bytes 3076
  22.3 19.4 %copy-start.3 = (f32[4,4]{1,0:T(4,128)S(1)}, f32[4,4]{1,0:T(4,128)}, u32[]{:S(2)}) copy-start(f32[4,4]{1,0:T(4,128)} %param.25) | copy-start | bytes 196
  22.3 238.1 %copy-start.4 = (s32[32]{0:T(128)S(1)}, s32[32]{0:T(128)}, u32[]{:S(2)}) copy-start(s32[32]{0:T(128)} %param.23) | copy-start | bytes 388
  22.3 238.1 %copy-start.5 = (s32[32]{0:T(128)S(1)}, s32[32]{0:T(128)}, u32[]{:S(2)}) copy-start(s32[32]{0:T(128)} %param.22) | copy-start | bytes 388
  22.3 238.1 %copy-start.7 = (f32[4]{0:T(128)S(1)}, f32[4]{0:T(128)}, u32[]{:S(2)}) copy-start(f32[4]{0:T(128)} %param.24) | copy-start | bytes 52
  22.3 244.1 %all-to-all-start = ((bf16[128,4,60,128]{3,1,2,0:T(4,128)(2,1)}), bf16[128,4,60,128]{3,1,2,0:T(4,128)(2,1)}, u32[]{:S(2)}, u32[]{:S(2)}) async-start(bf16[128,4,60,128]{3,1,2,0:T(4,128)(2,1)} %stack.8), calls=%async_computation | async-start | bytes 15728640 | tf_op jit(solution)/shard_map/all_to_all | solution.py:87
  35.4 226.4 %all-gather.2.cloned.1.call-start = ((), (), s32[]{:S(2)}) async-start(), calls=%async_computation.1 | async-start | bytes 2949120 | tf_op jit(solution)/shard_map/all_gather | solution.py:79
  266.4 8.6 %copy-start = (bf16[240,32,128]{2,1,0:T(8,128)(2,1)S(1)}, bf16[240,32,128]{2,1,0:T(8,128)(2,1)}, u32[]{:S(2)}) copy-start(bf16[240,32,128]{2,1,0:T(8,128)(2,1)} %reshape.83) | copy-start | bytes 5898244
  482.0 10.2 %copy-start.6 = (s32[8192]{0:T(1024)S(1)}, s32[8192]{0:T(1024)}, u32[]{:S(2)}) copy-start(s32[8192]{0:T(1024)} %param.17) | copy-start | bytes 98308
Sparse Core Ops, SparseCore 0:
  38.1 73.4 all-gather.1
